TPU v7x, 32 devices: a whole 2x2x4 slice. The times are simulated.
32 devices in a mesh: grp: 8 (over z, x), dev: 4 (over y, core).
Axes of the slice: x: 2, y: 2, z: 4, core: 2. Of those that a mesh axis runs over, the one named last changes fastest.
Arguments:
- block_states: float32 [256, 5, 4096], P(('grp', 'dev')), may hold values from -2 to 10.5, as said below
- dest_dev: int32 [256], P('grp'), may hold values from -1 to 3, as said below
- dest_slot: int32 [256], P('grp'), may hold values from 0 to 3, as said below
- neighbours: int32 [2, 128], P(None, 'grp'), may hold values from -1 to 15, as said below
- coarse_map: int32 [4, 32], P('dev'), may hold values from 0 to 31, each once within a row
Outputs:
- advanced: float32 [128, 5, 4096], P(('grp', 'dev'))
- registers: float32 [32, 5, 256], P(('grp', 'dev'))
Inputs may be any that keep to these rules, and one draw needn't show every extreme that they name: `block_states`: every slot holds a physical state: density 0.5 to 2, each velocity component -1 to 1, pressure 0.3 to 3. `dest_dev`: each pair of a receiving device index and a slot 0 .. 3 of a group gets exactly one patch; a device keeps its own patches or sends at most one patch to each of the next 3 device indices of its group (counted modulo 4) and to no other. `dest_slot`: see dest_dev. Index dev * 4 + slot within the group; neighbours are mutual (neighbours[1, a] = b exactly when neighbours[0, b] = a, within a group), a neighbour's index differs from the patch's own by at most 3, and -1 marks a domain boundary. `coarse_map`: for each device index a permutation: value m names register m // 4 in the group order, quadrant m % 4.
All inputs are finite; a program needn't handle non-finite values.
Results may differ from a plain program's by a relative error of at most 0.0003.
Values sent between devices are 32-bit elements; how exact they have to be, the bound alone decides.
No kernel may reach another device: no remote copies, remote signals or barrier semaphores. Data moves between devices by JAX's collectives and lax.ppermute only.
A program may use at most 64 MiB of HBM per device.

v0:
```python
import jax
import jax.numpy as jnp
from jax import lax
from jax.sharding import PartitionSpec as P

SIDE_LENGTH = 16
DEVICE_PATCHES = 4
P_DEV = 8


GAMMA = 1.4
COURANT = 0.2


def passed_along(block, axis, distance):
    devices = range(lax.axis_size(axis))
    route = [((i - distance) % len(devices), i) for i in devices]
    return lax.ppermute(block, axis, route)


def shifted(shard, axis, by):
    size = lax.axis_size(axis)
    pairs = [(i, i + by) for i in range(size) if 0 <= i + by < size]
    return lax.ppermute(shard, axis, pairs)


def primitives(conserved):
    density = conserved[..., 0, :, :]
    inverse = 1.0 / density
    vel_x = conserved[..., 1, :, :] * inverse
    vel_y = conserved[..., 2, :, :] * inverse
    vel_z = conserved[..., 3, :, :] * inverse
    kinetic = 0.5 * (
        conserved[..., 1, :, :] * vel_x
        + conserved[..., 2, :, :] * vel_y
        + conserved[..., 3, :, :] * vel_z
    )
    pressure = (GAMMA - 1.0) * (conserved[..., 4, :, :] - kinetic)
    return jnp.stack([density, vel_x, vel_y, vel_z, pressure], axis=-3)


def euler_flux(primitive):
    density = primitive[..., 0, :, :]
    vel_x = primitive[..., 1, :, :]
    vel_y = primitive[..., 2, :, :]
    vel_z = primitive[..., 3, :, :]
    pressure = primitive[..., 4, :, :]
    mass_flux = density * vel_x
    energy = pressure / (GAMMA - 1.0) + 0.5 * density * (
        vel_x * vel_x + vel_y * vel_y + vel_z * vel_z
    )
    fluxes = jnp.stack(
        [
            mass_flux,
            mass_flux * vel_x + pressure,
            mass_flux * vel_y,
            mass_flux * vel_z,
            vel_x * (energy + pressure),
        ],
        axis=-3,
    )
    conserved = jnp.stack([density, mass_flux, density * vel_y, density * vel_z, energy], axis=-3)
    speeds = jnp.abs(vel_x) + jnp.sqrt(GAMMA * pressure / density)
    return (fluxes, conserved, speeds)


def advance(block_volumes, lower_ghost, upper_ghost):
    extended = jnp.concatenate([lower_ghost, block_volumes, upper_ghost], axis=-2)
    primitive = primitives(extended)
    below_diff = primitive[..., 1:-1, :] - primitive[..., :-2, :]
    above_diff = primitive[..., 2:, :] - primitive[..., 1:-1, :]
    slopes = (
        0.5
        * (jnp.sign(below_diff) + jnp.sign(above_diff))
        * jnp.minimum(jnp.abs(below_diff), jnp.abs(above_diff))
    )
    centre = primitive[..., 1:-1, :]
    left_state = (centre + 0.5 * slopes)[..., :-1, :]
    right_state = (centre - 0.5 * slopes)[..., 1:, :]
    left_flux, left_cons, left_speed = euler_flux(left_state)
    right_flux, right_cons, right_speed = euler_flux(right_state)
    largest = jnp.maximum(left_speed, right_speed)[..., None, :, :]
    interface = 0.5 * (left_flux + right_flux) - 0.5 * largest * (right_cons - left_cons)
    updated = block_volumes - COURANT * (interface[..., 1:, :] - interface[..., :-1, :])
    return (updated, interface[..., -1, :])


def fill_edges(block_volumes, lower_ghost, upper_ghost, lower_nbr, upper_nbr):
    first = block_volumes[:, :, :1, :]
    last = block_volumes[:, :, -1:, :]
    lower_ghost = jnp.where(
        (lower_nbr < 0)[:, None, None, None], jnp.concatenate([first, first], axis=2), lower_ghost
    )
    upper_ghost = jnp.where(
        (upper_nbr < 0)[:, None, None, None], jnp.concatenate([last, last], axis=2), upper_ghost
    )
    return (lower_ghost, upper_ghost)


def coarsen(interface):
    half_edge = SIDE_LENGTH // 2
    shaped = interface.reshape(interface.shape[:-1] + (half_edge, 2, half_edge, 2))
    return shaped.mean(axis=(-3, -1))


def spread(coarse, quadrant):
    half_edge = SIDE_LENGTH // 2
    tiled = jnp.tile(coarse, (1,) * (coarse.ndim - 2) + (2, 2))
    row_ids = jnp.arange(SIDE_LENGTH, dtype=jnp.int32) // half_edge
    inside = (row_ids[:, None] == (quadrant // 2)[..., None, None]) & (
        row_ids[None, :] == (quadrant % 2)[..., None, None]
    )
    placed = tiled * inside.astype(tiled.dtype)[..., None, :, :]
    return placed.reshape(placed.shape[:-2] + (SIDE_LENGTH * SIDE_LENGTH,))


def selected_lines(weights, operand):
    flat = operand.reshape(operand.shape[0], -1)
    picked = jnp.dot(weights, flat, precision=lax.Precision.HIGHEST)
    return picked.reshape((weights.shape[0],) + operand.shape[1:])


def add_faces(totals, arrived, labels, lower_nbr, upper_nbr):
    below_sel = (lower_nbr[:, None] == labels[None, :]).astype(jnp.float32)
    above_sel = (upper_nbr[:, None] == labels[None, :]).astype(jnp.float32)
    return (
        totals[0] + selected_lines(below_sel, arrived[0]),
        totals[1] + selected_lines(above_sel, arrived[1]),
    )


def landing_rows(plan_dev, plan_slot, source_dev, my_dev, wanted):
    from_dev = lax.dynamic_index_in_dim(plan_dev, source_dev, 0, keepdims=False)
    from_slot = lax.dynamic_index_in_dim(plan_slot, source_dev, 0, keepdims=False)
    hits = (from_dev[None, :] == my_dev) & (from_slot[None, :] == wanted[:, None])
    return jnp.any(hits, axis=1).astype(jnp.float32)[:, None]


def local(block_states, dest_dev, dest_slot, neighbours, coarse_map):
    n_dev = lax.axis_size("dev")
    my_dev = lax.axis_index("dev")
    group_me = lax.axis_index("grp")
    cell_fields = block_states.shape[1]
    plane_cell_count = SIDE_LENGTH * SIDE_LENGTH
    wanted = jnp.arange(DEVICE_PATCHES, dtype=jnp.int32)
    mine_dev = lax.dynamic_slice_in_dim(dest_dev, my_dev * P_DEV, P_DEV)
    mine_slot = lax.dynamic_slice_in_dim(dest_slot, my_dev * P_DEV, P_DEV)
    retained_lines = (
        (mine_dev[None, :] == my_dev) & (mine_slot[None, :] == wanted[:, None])
    ).astype(jnp.float32)
    plan_dev = dest_dev.reshape(n_dev, P_DEV)
    plan_slot = dest_slot.reshape(n_dev, P_DEV)
    lower_all = neighbours[0]
    upper_all = neighbours[1]
    redistributed_blocks = selected_lines(retained_lines, block_states)
    for distance in range(1, DEVICE_PATCHES):
        target_dev = (my_dev + distance) % n_dev
        source_dev = (my_dev + n_dev - distance) % n_dev
        sending = (mine_dev == target_dev).astype(jnp.float32)[None, :]
        arrived = passed_along(selected_lines(sending, block_states), "dev", distance)
        redistributed_blocks = redistributed_blocks + selected_lines(
            landing_rows(plan_dev, plan_slot, source_dev, my_dev, wanted), arrived
        )
    block_volumes = redistributed_blocks.reshape(
        DEVICE_PATCHES, cell_fields, SIDE_LENGTH, plane_cell_count
    )
    lower_nbr = lax.dynamic_slice_in_dim(lower_all, my_dev * DEVICE_PATCHES, DEVICE_PATCHES)
    upper_nbr = lax.dynamic_slice_in_dim(upper_all, my_dev * DEVICE_PATCHES, DEVICE_PATCHES)
    top_layers = block_volumes[:, :, SIDE_LENGTH - 2 :, :]
    bottom_layers = block_volumes[:, :, :2, :]
    empty = jnp.zeros((DEVICE_PATCHES, cell_fields, 2, plane_cell_count), jnp.float32)
    ghosts = add_faces(
        (empty, empty),
        (top_layers, bottom_layers),
        my_dev * DEVICE_PATCHES + wanted,
        lower_nbr,
        upper_nbr,
    )
    from_below = shifted((top_layers, bottom_layers), "dev", 1)
    labels_below = jnp.where(my_dev > 0, (my_dev - 1) * DEVICE_PATCHES + wanted, -3)
    ghosts = add_faces(ghosts, from_below, labels_below, lower_nbr, upper_nbr)
    from_above = shifted((top_layers, bottom_layers), "dev", -1)
    labels_above = jnp.where(my_dev < n_dev - 1, (my_dev + 1) * DEVICE_PATCHES + wanted, -3)
    ghosts = add_faces(ghosts, from_above, labels_above, lower_nbr, upper_nbr)
    lower_ghost, upper_ghost = ghosts
    lower_ghost, upper_ghost = fill_edges(
        block_volumes, lower_ghost, upper_ghost, lower_nbr, upper_nbr
    )
    advanced, interface = advance(block_volumes, lower_ghost, upper_ghost)
    out_state = advanced.reshape(DEVICE_PATCHES, cell_fields, SIDE_LENGTH**3)
    column = coarse_map[0]
    half_edge = SIDE_LENGTH // 2
    coarse = coarsen(interface).reshape(DEVICE_PATCHES, cell_fields * half_edge * half_edge)
    arrived = lax.all_gather(coarse, "grp", axis=0, tiled=True)
    matched = (column // DEVICE_PATCHES == group_me).astype(jnp.float32)
    placed = spread(
        arrived.reshape(arrived.shape[0], cell_fields, half_edge, half_edge),
        column % DEVICE_PATCHES,
    )
    registers = jnp.einsum("k,kfc->fc", matched, placed, precision=lax.Precision.HIGHEST)[None]
    return (out_state, registers)


def solution(mesh):
    in_specs = (P(("grp", "dev"), None, None), P("grp"), P("grp"), P(None, "grp"), P("dev", None))
    out_specs = (P(("grp", "dev"), None, None), P(("grp", "dev"), None, None))
    return jax.shard_map(local, mesh=mesh, in_specs=in_specs, out_specs=out_specs, check_vma=False)
```

profile of v0, /device:TPU:0, one launch (start us, length us, event | category | flops | bytes accessed | tf_op | source)
XLA Modules:
  0.0 61.7 jit_solution(8667873022805380065)
XLA Ops:
  0.7 0.7 %copy-done.1 = s32[32]{0:T(128)S(1)} copy-done((s32[32]{0:T(128)S(1)}, s32[32]{0:T(128)}, u32[]{:S(2)}) %copy-start.1) | copy-done | bytes 152
  1.5 0.3 copy-done
  1.7 0.4 fusion.2
  2.2 2.5 %collective-permute-start.2 = (f32[1,5,4096]{2,1,0:T(8,128)S(1)}, f32[1,5,4096]{2,1,0:T(8,128)S(1)}, u32[]{:S(2)}, u32[]{:S(2)}) collective-permute-start(f32[1,5,4096]{2,1,0:T(8,128)S(1)} %copy.68), channel_id=1, source_target_pairs={{1,0},{2,1},{3,2},{0,3},{5,4},{6,5},{7,6},{4,7},{9,8},{10,9},{11,1... | collective-permute-start | bytes 245768 | tf_op jit(solution)/shard_map/ppermute | solution.py:18
  4.7 0.4 fusion.4
  5.2 0.7 %collective-permute-start.1 = (f32[1,5,4096]{2,1,0:T(8,128)S(1)}, f32[1,5,4096]{2,1,0:T(8,128)S(1)}, u32[]{:S(2)}, u32[]{:S(2)}) collective-permute-start(f32[1,5,4096]{2,1,0:T(8,128)S(1)} %copy.67), channel_id=1, source_target_pairs={{2,0},{3,1},{0,2},{1,3},{6,4},{7,5},{4,6},{5,7},{10,8},{11,9},{8,1... | collective-permute-start | bytes 245768 | tf_op jit(solution)/shard_map/ppermute | solution.py:18
  5.8 0.4 fusion.6
  6.7 0.6 copy-done.4
  7.8 0.7 %copy-done.2 = s32[2,16]{1,0:T(2,128)S(1)} copy-done((s32[2,16]{1,0:T(2,128)S(1)}, s32[2,16]{1,0:T(2,128)}, u32[]{:S(2)}) %copy-start.2) | copy-done | bytes 152
  8.6 0.6 copy-done.3
  9.4 2.7 %collective-permute-done.1 = f32[1,5,4096]{2,1,0:T(8,128)S(1)} collective-permute-done((f32[1,5,4096]{2,1,0:T(8,128)S(1)}, f32[1,5,4096]{2,1,0:T(8,128)S(1)}, u32[]{:S(2)}, u32[]{:S(2)}) %collective-permute-start.1) | collective-permute-done | bytes 81952 | tf_op jit(solution)/shard_map/ppermute | solution.py:18
  12.1 0.4 collective-permute-done
  12.4 0.5 multiply_add_fusion
  13.3 1.3 %collective-permute-start.5 = (f32[4,5,2,256]{3,2,1,0:T(2,128)S(1)}, f32[4,5,2,256]{3,2,1,0:T(2,128)S(1)}, u32[]{:S(2)}, u32[]{:S(2)}) collective-permute-start(f32[4,5,2,256]{3,2,1,0:T(2,128)S(1)} %copy.77), channel_id=1, source_target_pairs={{0,1},{1,2},{2,3},{4,5},{5,6},{6,7},{8,9},{9,10},{10,11},{12,13},{... | collective-permute-start | bytes 122888 | tf_op jit(solution)/shard_map/ppermute | solution.py:24
  14.6 1.3 %collective-permute-start.6 = (f32[4,5,2,256]{3,2,1,0:T(2,128)S(1)}, f32[4,5,2,256]{3,2,1,0:T(2,128)S(1)}, u32[]{:S(2)}, u32[]{:S(2)}) collective-permute-start(f32[4,5,2,256]{3,2,1,0:T(2,128)S(1)} %copy.77), channel_id=1, source_target_pairs={{1,0},{2,1},{3,2},{5,4},{6,5},{7,6},{9,8},{10,9},{11,10},{13,12},{... | collective-permute-start | bytes 122888 | tf_op jit(solution)/shard_map/ppermute | solution.py:24
  15.9 4.7 %collective-permute-start.3 = (f32[4,5,2,256]{3,2,1,0:T(2,128)S(1)}, f32[4,5,2,256]{3,2,1,0:T(2,128)S(1)}, u32[]{:S(2)}, u32[]{:S(2)}) collective-permute-start(f32[4,5,2,256]{3,2,1,0:T(2,128)S(1)} %copy.76), channel_id=1, source_target_pairs={{0,1},{1,2},{2,3},{4,5},{5,6},{6,7},{8,9},{9,10},{10,11},{12,13},{... | collective-permute-start | bytes 122888 | tf_op jit(solution)/shard_map/ppermute | solution.py:24
  20.7 1.3 %collective-permute-start.4 = (f32[4,5,2,256]{3,2,1,0:T(2,128)S(1)}, f32[4,5,2,256]{3,2,1,0:T(2,128)S(1)}, u32[]{:S(2)}, u32[]{:S(2)}) collective-permute-start(f32[4,5,2,256]{3,2,1,0:T(2,128)S(1)} %copy.76), channel_id=1, source_target_pairs={{1,0},{2,1},{3,2},{5,4},{6,5},{7,6},{9,8},{10,9},{11,10},{13,12},{... | collective-permute-start | bytes 122888 | tf_op jit(solution)/shard_map/ppermute | solution.py:24
  23.3 1.7 %collective-permute-done.4 = f32[4,5,2,256]{3,2,1,0:T(2,128)S(1)} collective-permute-done((f32[4,5,2,256]{3,2,1,0:T(2,128)S(1)}, f32[4,5,2,256]{3,2,1,0:T(2,128)S(1)}, u32[]{:S(2)}, u32[]{:S(2)}) %collective-permute-start.4) | collective-permute-done | bytes 40992 | tf_op jit(solution)/shard_map/ppermute | solution.py:24
  25.7 0.4 slice_add_fusion
  27.1 0.8 %fusion.11 = f32[4,5,16,256]{3,0,2,1:T(4,128)} fusion(f32[4,5,16,256]{3,0,2,1:T(4,128)S(1)} %bitcast.134, f32[4,5,17,256]{3,0,2,1:T(4,128)S(1)} %multiply_subtract_fusion), kind=kLoop, calls=%fused_computation.21 | loop fusion | flops 245760 | bytes 1310720 | tf_op jit(solution)/shard_map/sub | solution.py:84
  28.2 0.4 reduce_sum.9
  29.0 31.1 %all-gather = f32[8,4,320]{2,1,0:T(4,128)S(1)} all-gather(f32[1,4,320]{2,1,0:T(4,128)S(1)} %reshape.347), channel_id=1, replica_groups=mesh['grp'=8,'dev'=4] {'grp'}, dimensions={0}, use_global_device_ids=true | all-gather | bytes 46080 | tf_op jit(solution)/shard_map/all_gather | solution.py:194
  60.7 0.4 fusion.27
  61.1 0.6 %broadcast_in_dim.19 = f32[1,5,256]{2,0,1:T(1,128)} reshape(f32[5,256]{1,0:T(8,128)S(1)} %bitcast.147) | data formatting | bytes 10240 | tf_op jit(solution)/shard_map/broadcast_in_dim | solution.py:200
  (84 shorter events, 5.7 us)
Async XLA Ops:
  0.6 1.1 %copy-start = (f32[8,5,4096]{2,0,1:T(8,128)S(1)}, f32[8,5,4096]{2,0,1:T(8,128)}, u32[]{:S(2)}) copy-start(f32[8,5,4096]{2,0,1:T(8,128)} %param.5) | copy-start | bytes 1966084
  0.7 0.7 %copy-start.1 = (s32[32]{0:T(128)S(1)}, s32[32]{0:T(128)}, u32[]{:S(2)}) copy-start(s32[32]{0:T(128)} %param.6) | copy-start | bytes 388
  2.2 7.1 %collective-permute-start.2 = (f32[1,5,4096]{2,1,0:T(8,128)S(1)}, f32[1,5,4096]{2,1,0:T(8,128)S(1)}, u32[]{:S(2)}, u32[]{:S(2)}) collective-permute-start(f32[1,5,4096]{2,1,0:T(8,128)S(1)} %copy.68), channel_id=1, source_target_pairs={{1,0},{2,1},{3,2},{0,3},{5,4},{6,5},{7,6},{4,7},{9,8},{10,9},{11,1... | collective-permute-start | bytes 245768 | tf_op jit(solution)/shard_map/ppermute | solution.py:18
  5.2 6.9 %collective-permute-start.1 = (f32[1,5,4096]{2,1,0:T(8,128)S(1)}, f32[1,5,4096]{2,1,0:T(8,128)S(1)}, u32[]{:S(2)}, u32[]{:S(2)}) collective-permute-start(f32[1,5,4096]{2,1,0:T(8,128)S(1)} %copy.67), channel_id=1, source_target_pairs={{2,0},{3,1},{0,2},{1,3},{6,4},{7,5},{4,6},{5,7},{10,8},{11,9},{8,1... | collective-permute-start | bytes 245768 | tf_op jit(solution)/shard_map/ppermute | solution.py:18
  6.3 6.1 %collective-permute-start = (f32[1,5,4096]{2,1,0:T(8,128)S(1)}, f32[1,5,4096]{2,1,0:T(8,128)S(1)}, u32[]{:S(2)}, u32[]{:S(2)}) collective-permute-start(f32[1,5,4096]{2,1,0:T(8,128)S(1)} %copy.66), channel_id=1, source_target_pairs={{3,0},{0,1},{1,2},{2,3},{7,4},{4,5},{5,6},{6,7},{11,8},{8,9},{9,10... | collective-permute-start | bytes 245768 | tf_op jit(solution)/shard_map/ppermute | solution.py:18
  6.6 0.7 %copy-start.4 = (s32[32]{0:T(128)S(1)}, s32[32]{0:T(128)}, u32[]{:S(2)}) copy-start(s32[32]{0:T(128)} %param.7) | copy-start | bytes 388
  7.8 0.7 %copy-start.2 = (s32[2,16]{1,0:T(2,128)S(1)}, s32[2,16]{1,0:T(2,128)}, u32[]{:S(2)}) copy-start(s32[2,16]{1,0:T(2,128)} %param.8) | copy-start | bytes 388
  8.5 0.7 %copy-start.3 = (s32[1,32]{1,0:T(1,128)S(1)}, s32[1,32]{1,0:T(1,128)}, u32[]{:S(2)}) copy-start(s32[1,32]{1,0:T(1,128)} %param.9) | copy-start | bytes 388
  13.3 9.2 %collective-permute-start.5 = (f32[4,5,2,256]{3,2,1,0:T(2,128)S(1)}, f32[4,5,2,256]{3,2,1,0:T(2,128)S(1)}, u32[]{:S(2)}, u32[]{:S(2)}) collective-permute-start(f32[4,5,2,256]{3,2,1,0:T(2,128)S(1)} %copy.77), channel_id=1, source_target_pairs={{0,1},{1,2},{2,3},{4,5},{5,6},{6,7},{8,9},{9,10},{10,11},{12,13},{... | collective-permute-start | bytes 122888 | tf_op jit(solution)/shard_map/ppermute | solution.py:24
  14.6 8.2 %collective-permute-start.6 = (f32[4,5,2,256]{3,2,1,0:T(2,128)S(1)}, f32[4,5,2,256]{3,2,1,0:T(2,128)S(1)}, u32[]{:S(2)}, u32[]{:S(2)}) collective-permute-start(f32[4,5,2,256]{3,2,1,0:T(2,128)S(1)} %copy.77), channel_id=1, source_target_pairs={{1,0},{2,1},{3,2},{5,4},{6,5},{7,6},{9,8},{10,9},{11,10},{13,12},{... | collective-permute-start | bytes 122888 | tf_op jit(solution)/shard_map/ppermute | solution.py:24
  15.9 7.1 %collective-permute-start.3 = (f32[4,5,2,256]{3,2,1,0:T(2,128)S(1)}, f32[4,5,2,256]{3,2,1,0:T(2,128)S(1)}, u32[]{:S(2)}, u32[]{:S(2)}) collective-permute-start(f32[4,5,2,256]{3,2,1,0:T(2,128)S(1)} %copy.76), channel_id=1, source_target_pairs={{0,1},{1,2},{2,3},{4,5},{5,6},{6,7},{8,9},{9,10},{10,11},{12,13},{... | collective-permute-start | bytes 122888 | tf_op jit(solution)/shard_map/ppermute | solution.py:24
  20.7 4.4 %collective-permute-start.4 = (f32[4,5,2,256]{3,2,1,0:T(2,128)S(1)}, f32[4,5,2,256]{3,2,1,0:T(2,128)S(1)}, u32[]{:S(2)}, u32[]{:S(2)}) collective-permute-start(f32[4,5,2,256]{3,2,1,0:T(2,128)S(1)} %copy.76), channel_id=1, source_target_pairs={{1,0},{2,1},{3,2},{5,4},{6,5},{7,6},{9,8},{10,9},{11,10},{13,12},{... | collective-permute-start | bytes 122888 | tf_op jit(solution)/shard_map/ppermute | solution.py:24
where the time goes:
time: 62 us; the launch traced here: 61.7 us
  blocking collectives  31.1 us (50%)
  starting transfers between devices  12 us (19%)
  local copies, waits for them, and re-layouts  5.52 us (9%)
  waiting for transfers between devices  4.78 us (8%)
  other arithmetic  3.65 us (6%)
  matrix products  3.52 us (6%)
  between operations  1.14 us (2%)
    all_gather x1, blocking collectives, local(): arrived = lax.all_gather(coarse, 'grp', axis=0, tiled=True)  31.1 us
    ppermute x4, starting transfers between devices, shifted(): return lax.ppermute(shard, axis, pairs)  8.6 us
    ppermute x3, starting transfers between devices, passed_along(): return lax.ppermute(block, axis, route)  3.39 us
    dot_general x10, matrix products, selected_lines(): picked = jnp.dot(weights, flat, precision=lax.Precision.HIGHEST)  3.09 us
    ppermute x3, waiting for transfers between devices, passed_along(): return lax.ppermute(block, axis, route)  3.08 us
    unnamed x16, local copies, waits for them, and re-layouts  2.97 us
    ppermute x4, waiting for transfers between devices, shifted(): return lax.ppermute(shard, axis, pairs)  1.69 us
  transfers between devices with their start and end apart: 7, of which 3 were waited for; matrix products, arithmetic and copies ran while one was open for 5% of the time, Pallas kernels for 0%

commit v1 on v0

v1 whole, which is shorter than its diff:
```python
import functools

import jax
import jax.numpy as jnp
from jax import lax
from jax.experimental import pallas as pl
from jax.experimental.pallas import tpu as pltpu
from jax.sharding import PartitionSpec as P

SIDE = 16
FIELDS = 5
KEEP = 4
REACH = 4
LANES = 128
HALVES = SIDE * SIDE // LANES
TILES = SIDE * HALVES
GROUP = HALVES * KEEP
GHOST = FIELDS * 2 * GROUP
TOPS = FIELDS * 2 * HALVES
PATCH = FIELDS * TILES
COARSE = 16

GAMMA = 1.4
COURANT = 0.2

VMEM = pl.BlockSpec(memory_space=pltpu.VMEM)
SMEM = pl.BlockSpec(memory_space=pltpu.SMEM)
HBM = pl.BlockSpec(memory_space=pltpu.HBM)


def rows(count):
    return jax.ShapeDtypeStruct((count, LANES), jnp.float32)


def params():
    return pltpu.CompilerParams(vmem_limit_bytes=8 * 1024 * 1024)


def primitives(u):
    inverse = 1.0 / u[0]
    vx, vy, vz = u[1] * inverse, u[2] * inverse, u[3] * inverse
    kinetic = 0.5 * (u[1] * vx + u[2] * vy + u[3] * vz)
    return [u[0], vx, vy, vz, (GAMMA - 1.0) * (u[4] - kinetic)]


def half_slopes(below, above):
    return [
        0.5 * (jnp.maximum(jnp.minimum(a, b), 0.0) + jnp.minimum(jnp.maximum(a, b), 0.0))
        for a, b in zip(below, above)
    ]


def euler_flux(state):
    r, vx, vy, vz, p = state
    mass = r * vx
    energy = p * (1.0 / (GAMMA - 1.0)) + 0.5 * r * (vx * vx + vy * vy + vz * vz)
    flux = [mass, mass * vx + p, mass * vy, mass * vz, vx * (energy + p)]
    conserved = [r, mass, r * vy, r * vz, energy]
    return flux, conserved, jnp.abs(vx) + jnp.sqrt(GAMMA * p / r)


def interface_flux(left, right):
    lf, lc, ls = euler_flux(left)
    rf, rc, rs = euler_flux(right)
    half = 0.5 * jnp.maximum(ls, rs)
    return [0.5 * (a + b) - half * (d - c) for a, b, c, d in zip(lf, rf, lc, rc)]


def pack_kernel(n, slots, deltas, dev_hbm, slot_hbm, nbr_hbm, x_hbm, *refs):
    count = len(deltas)
    early = refs[:count]
    late = refs[count : 2 * count]
    own, x, plan, dev, slot, nbr, inv, sems = refs[2 * count :]
    copies = [
        pltpu.make_async_copy(src, dst, sems.at[i])
        for i, (src, dst) in enumerate(
            ((x_hbm, x), (dev_hbm, dev), (slot_hbm, slot), (nbr_hbm, nbr))
        )
    ]
    for copy in copies:
        copy.start()
    me = lax.axis_index("dev")
    total = n * slots
    for copy in copies[1:]:
        copy.wait()

    def invert(i, carry):
        to = dev[i]
        inv[jnp.where(to >= 0, to * KEEP + slot[i], n * KEEP)] = i
        return carry

    if total <= 64:
        for i in range(total):
            invert(i, 0)
    else:
        lax.fori_loop(0, total, invert, 0)

    def held(p):
        i = inv[p]
        holder = lax.div(i, slots)
        return holder == me, lax.rem(i, slots), holder

    def ghost(side, p, mine, at):
        near = nbr[side, p]
        edge = near < 0
        nbr_mine, nbr_at, _ = held(jnp.maximum(near, 0))
        valid = jnp.where(edge, mine, nbr_mine).astype(jnp.float32)
        first, second = (TILES - 2 * HALVES, TILES - HALVES) if side == 0 else (0, HALVES)
        flat = 0 if side == 0 else TILES - HALVES
        source = jnp.where(edge, at, nbr_at)
        return (
            valid,
            jnp.where(edge, flat, first) * slots + source,
            jnp.where(edge, flat, second) * slots + source,
        )

    wanted = []
    for delta in (0,) + deltas:
        c = me + delta
        c = jnp.where(c >= n, c - n, c)
        label, patch_at = jnp.float32(-1.0), jnp.int32(0)
        faces = []
        for q in range(KEEP):
            p = c * KEEP + q
            mine, at, holder = held(p)
            label = jnp.where(mine, jnp.float32(q), label)
            patch_at = jnp.where(mine, at, patch_at)
            faces.append((mine, at, ghost(0, p, mine, at), ghost(1, p, mine, at)))
            if delta == 0:
                away = me - holder
                plan[q] = jnp.where(away < 0, away + n, away)
                plan[KEEP + q] = at
        wanted.append((label, patch_at, faces))
    copies[0].wait()

    def put_ghost(ref, base, q, where):
        valid, first, second = where
        for f in range(FIELDS):
            at = f * TILES * slots
            for layer, start in enumerate((first, second)):
                v = x[pl.ds(at + start, HALVES, stride=slots), :] * valid
                ref[pl.ds(base + (f * 2 + layer) * GROUP + q, HALVES, stride=KEEP), :] = v

    top = (TILES - 2 * HALVES) * slots
    for k, delta in enumerate(deltas):
        label, patch_at, faces = wanted[1 + k]
        for q in range(KEEP):
            put_ghost(early[k], 0, q, faces[q][3])
        if delta < REACH:
            for f in range(FIELDS):
                early[k][pl.ds(GHOST + f * 2 * HALVES, 2 * HALVES), :] = x[
                    pl.ds(f * TILES * slots + top + patch_at, 2 * HALVES, stride=slots), :
                ]
            early[k][pl.ds(GHOST + TOPS, 4), :] = jnp.full((4, LANES), label, jnp.float32)
    for k, delta in enumerate(deltas):
        _, patch_at, faces = wanted[1 + k]
        base = 0
        if delta < REACH:
            base = PATCH
            for t in range(0, PATCH, 8):
                late[k][pl.ds(t, 8), :] = x[pl.ds(t * slots + patch_at, 8, stride=slots), :]
        for q in range(KEEP):
            put_ghost(late[k], base, q, faces[q][2])
    for q, (mine, at, lower, upper) in enumerate(wanted[0][2]):
        kept = mine.astype(jnp.float32)
        put_ghost(own, 0, q, (kept, top + at, top + HALVES * slots + at))
        put_ghost(own, GHOST, q, upper)
        put_ghost(own, 2 * GHOST, q, lower)


def layer(ref, base, f, number):
    return ref[pl.ds(base + (f * 2 + number) * GROUP, GROUP), :]


def coarse_kernel(deltas, *refs):
    early = refs[: len(deltas)]
    own, out = refs[len(deltas) :]
    row = lax.broadcasted_iota(jnp.int32, (GROUP, LANES), 0)
    lane = lax.broadcasted_iota(jnp.int32, (GROUP, LANES), 1)
    which = lax.rem(row, KEEP)
    half = lax.div(row, KEEP)
    place = which.astype(jnp.float32)
    patches = [
        (e, jnp.broadcast_to(e[pl.ds(GHOST + TOPS, 1), :], (GROUP, LANES)) == place)
        for e, delta in zip(early, deltas)
        if delta < REACH
    ]

    def top_layer(f, number):
        total = layer(own, 0, f, number)
        for e, mask in patches:
            at = GHOST + (f * 2 + number) * HALVES
            v = jnp.where(half == 0, e[pl.ds(at, 1), :], e[pl.ds(at + 1, 1), :])
            total = total + jnp.where(mask, v, 0.0)
        return total

    def upper_layer(f, number):
        total = layer(own, GHOST, f, number)
        for e in early:
            total = total + layer(e, 0, f, number)
        return total

    a0, a1 = (primitives([top_layer(f, i) for f in range(FIELDS)]) for i in range(2))
    b0, b1 = (primitives([upper_layer(f, i) for f in range(FIELDS)]) for i in range(2))
    d0 = [b - a for a, b in zip(a0, a1)]
    d1 = [b - a for a, b in zip(a1, b0)]
    d2 = [b - a for a, b in zip(b0, b1)]
    left = [a + s for a, s in zip(a1, half_slopes(d0, d1))]
    right = [b - s for b, s in zip(b0, half_slopes(d1, d2))]
    flux = jnp.concatenate(interface_flux(left, right), axis=0)
    fine = lax.broadcasted_iota(jnp.int32, (LANES, LANES), 0)
    spot = lax.broadcasted_iota(jnp.int32, (LANES, LANES), 1)
    edge = SIDE // 2
    same_y = lax.div(fine, 2 * SIDE) == lax.rem(lax.div(spot, SIDE), edge // 2)
    same_z = lax.rem(lax.div(fine, 2), edge) == lax.rem(spot, edge)
    mean = jnp.where(same_y & same_z, 0.25, 0.0)
    spread = jnp.dot(
        flux, mean, precision=lax.Precision.HIGHEST, preferred_element_type=jnp.float32
    )
    keep = (lax.div(lane, LANES // HALVES) == half) & (
        lax.rem(lax.div(lane, edge), 2) == lax.rem(which, 2)
    )
    out[...] = jnp.zeros_like(out)
    for f in range(FIELDS):
        v = jnp.where(keep, spread[f * GROUP : (f + 1) * GROUP], 0.0)
        v = v[:KEEP] + v[KEEP:]
        out[pl.ds(2 * f, 1), :] = v[0:1] + v[1:2]
        out[pl.ds(2 * f + 1, 1), :] = v[2:3] + v[3:4]


def step_kernel(n, slots, groups, butterfly, deltas, plan, cmap, x, own, *refs):
    count = len(deltas)
    early = refs[:count]
    late = refs[count : 2 * count]
    out, codes, ext = refs[2 * count :]
    span = (SIDE + 4) * GROUP
    lows = [PATCH if delta < REACH else 0 for delta in deltas]
    for f in range(FIELDS):
        for number in range(2):
            lower = layer(own, 2 * GHOST, f, number)
            upper = layer(own, GHOST, f, number)
            for e, v, low in zip(early, late, lows):
                lower = lower + layer(v, low, f, number)
                upper = upper + layer(e, 0, f, number)
            ext[pl.ds(f * span + number * GROUP, GROUP), :] = lower
            ext[pl.ds(f * span + (SIDE + 2 + number) * GROUP, GROUP), :] = upper
    for q in range(KEEP):
        source, at = plan[q], plan[KEEP + q]

        def fill(read, q=q):
            for f in range(FIELDS):
                for t in range(0, TILES, 8):
                    to = f * span + 2 * GROUP + t * KEEP + q
                    ext[pl.ds(to, 8, stride=KEEP), :] = read(f * TILES + t)

        @pl.when(source == 0)
        def _():
            fill(lambda t: x[pl.ds(t * slots + at, 8, stride=slots), :])

        for delta, ref in zip(deltas, late):
            if delta < REACH:

                @pl.when(source == delta)
                def _(ref=ref):
                    fill(lambda t: ref[pl.ds(t, 8), :])

    def cells(k):
        return [ext[pl.ds(f * span + k * GROUP, GROUP), :] for f in range(FIELDS)]

    p0, p1 = primitives(cells(0)), primitives(cells(1))
    mid = primitives(cells(2))
    below = [b - a for a, b in zip(p0, p1)]
    above = [b - a for a, b in zip(p1, mid)]
    left = [a + s for a, s in zip(p1, half_slopes(below, above))]
    before = None
    for j in range(SIDE + 1):
        ahead = primitives(cells(j + 3))
        diff = [b - a for a, b in zip(mid, ahead)]
        slopes = half_slopes(above, diff)
        right = [a - s for a, s in zip(mid, slopes)]
        flux = interface_flux(left, right)
        if before is not None:
            u = cells(j + 1)
            for f in range(FIELDS):
                v = u[f] - COURANT * (flux[f] - before[f])
                for h in range(HALVES):
                    out[f, (j - 1) * HALVES + h] = v[h * KEEP : (h + 1) * KEEP]
        left = [a + s for a, s in zip(mid, slopes)]
        before, mid, above = flux, ahead, diff

    me = lax.axis_index("grp")
    odd = lax.rem(lax.div(lax.broadcasted_iota(jnp.int32, (1, LANES), 1), SIDE // 2), 2) == 1
    for r in range(groups):
        g = lax.bitwise_xor(me, r) if butterfly else jnp.int32(r)
        quadrant = []
        for q in range(KEEP):
            m = cmap[0, g * KEEP + q]
            quadrant.append(jnp.where(lax.div(m, KEEP) == me, lax.rem(m, KEEP), -1))
        for pair in range(2):
            codes[pl.ds(pair * groups + r, 1), :] = jnp.where(
                odd, quadrant[2 * pair + 1], quadrant[2 * pair]
            )


def register_kernel(groups, faces, codes, out):
    edge = SIDE // 2
    lane = lax.broadcasted_iota(jnp.int32, (8, LANES), 1)
    odd = lax.rem(lax.div(lane, edge), 2)
    for f in range(FIELDS):
        sums = [jnp.zeros((8, LANES), jnp.float32) for _ in range(4)]
        for r in range(0, groups, 8):
            for pair in range(2):
                v = faces[pl.ds(r * COARSE + 2 * f + pair, 8, stride=COARSE), :]
                code = codes[pl.ds(pair * groups + r, 8), :]
                sums = [s + jnp.where(code == t, v, 0.0) for t, s in enumerate(sums)]
        for h in range(HALVES):
            even_q, odd_q = sums[2 * h], sums[2 * h + 1]
            even_q = even_q + pltpu.roll(even_q, LANES - edge, 1)
            odd_q = odd_q + pltpu.roll(odd_q, edge, 1)
            v = jnp.where(odd == 0, even_q, odd_q)
            out[f, :, pl.ds(h * LANES, LANES)] = jnp.sum(v, axis=0, keepdims=True)


def exchange(block, groups):
    stride = 1
    while stride < groups:
        route = [(i, i ^ stride) for i in range(groups)]
        block = jnp.concatenate([block, lax.ppermute(block, "grp", route)], axis=0)
        stride *= 2
    return block


def local(block_states, dest_dev, dest_slot, neighbours, coarse_map):
    n = lax.axis_size("dev")
    groups = lax.axis_size("grp")
    slots = block_states.shape[0]
    deltas = tuple(sorted({delta % n for delta in range(-1, REACH + 1)} - {0}))
    butterfly = groups & (groups - 1) == 0
    x = block_states.reshape(slots, FIELDS, TILES, LANES).transpose(1, 2, 0, 3)
    x = x.reshape(FIELDS * TILES * slots, LANES)
    early_rows = [GHOST + (TOPS + 4 if delta < REACH else 0) for delta in deltas]
    late_rows = [GHOST + (PATCH if delta < REACH else 0) for delta in deltas]
    count = len(deltas)
    *sent, own, x, plan = pl.pallas_call(
        functools.partial(pack_kernel, n, slots, deltas),
        out_shape=[rows(r) for r in early_rows + late_rows]
        + [rows(3 * GHOST), rows(x.shape[0]), jax.ShapeDtypeStruct((2 * KEEP,), jnp.int32)],
        in_specs=[HBM] * 4,
        out_specs=[VMEM] * (2 * count + 2) + [SMEM],
        scratch_shapes=[
            pltpu.SMEM(dest_dev.shape, jnp.int32),
            pltpu.SMEM(dest_slot.shape, jnp.int32),
            pltpu.SMEM(neighbours.shape, jnp.int32),
            pltpu.SMEM((n * KEEP + 1,), jnp.int32),
            pltpu.SemaphoreType.DMA((4,)),
        ],
        compiler_params=params(),
        name="pack",
    )(dest_dev, dest_slot, neighbours, x)
    routes = [[(i, (i + delta) % n) for i in range(n)] for delta in deltas]
    order = range(count - 1, -1, -1)
    early, late = [None] * count, [None] * count
    for k in order:
        early[k] = lax.ppermute(sent[k], "dev", routes[k])
    for k in order:
        late[k] = lax.ppermute(sent[count + k], "dev", routes[k])
    faces = pl.pallas_call(
        functools.partial(coarse_kernel, deltas),
        out_shape=rows(COARSE),
        in_specs=[VMEM] * (count + 1),
        out_specs=VMEM,
        compiler_params=params(),
        name="coarse",
    )(*early, own)
    if butterfly:
        faces = exchange(faces, groups)
    else:
        faces = lax.all_gather(faces, "grp", axis=0, tiled=True)
    advanced, codes = pl.pallas_call(
        functools.partial(step_kernel, n, slots, groups, butterfly, deltas),
        out_shape=[
            jax.ShapeDtypeStruct((FIELDS, TILES, KEEP, LANES), jnp.float32),
            jax.ShapeDtypeStruct((2 * groups, LANES), jnp.int32),
        ],
        in_specs=[SMEM, SMEM] + [VMEM] * (2 + 2 * count),
        out_specs=[VMEM, VMEM],
        scratch_shapes=[pltpu.VMEM((FIELDS * (SIDE + 4) * GROUP, LANES), jnp.float32)],
        compiler_params=params(),
        name="step",
    )(plan, coarse_map, x, own, *early, *late)
    registers = pl.pallas_call(
        functools.partial(register_kernel, groups),
        out_shape=jax.ShapeDtypeStruct((FIELDS, 1, SIDE * SIDE), jnp.float32),
        in_specs=[VMEM, VMEM],
        out_specs=VMEM,
        compiler_params=params(),
        name="registers",
    )(faces, codes)
    advanced = advanced.transpose(2, 0, 1, 3).reshape(KEEP, FIELDS, TILES * LANES)
    return (advanced, registers.transpose(1, 0, 2))


def solution(mesh):
    in_specs = (P(("grp", "dev"), None, None), P("grp"), P("grp"), P(None, "grp"), P("dev", None))
    out_specs = (P(("grp", "dev"), None, None), P(("grp", "dev"), None, None))
    return jax.shard_map(local, mesh=mesh, in_specs=in_specs, out_specs=out_specs, check_vma=False)
```

time: 62 us -> 32.8 us (0.53)
  blocking collectives: 31.1 us -> 0 us
  waiting for transfers between devices: 4.78 us -> 10.4 us
  Pallas kernels: 0 us -> 4.96 us
  other arithmetic: 3.65 us -> 0.01 us
  matrix products: 3.52 us -> 0 us
  local copies, waits for them, and re-layouts: 5.52 us -> 3.08 us
  starting transfers between devices: 12 us -> 13.2 us
    all_gather x1 -> x0, blocking collectives: 31.1 us -> none  [local(): arrived = lax.all_gather(coarse, 'grp', axis=0, tiled=True)]
    ppermute x7 -> x9, waiting for transfers between devices: 4.78 us -> 10.4 us  [the longest x3 4.32 us: exchange(): block = jnp.concatenate([block, lax.ppermute(block, 'grp', route)], axis=0)]
    pallas_call x0 -> x4, Pallas kernels: none -> 4.96 us  [the longest x1 2.14 us: local(): pl.pallas_call(functools.partial(pack_kernel, n, slots, deltas), out_shap...]
    dot_general x11 -> x0, matrix products: 3.52 us -> none  [the longest x10 3.09 us: selected_lines(): picked = jnp.dot(weights, flat, precision=lax.Precision.HIGHEST)]
    sub x3 -> x0, other arithmetic: 1.17 us -> none  [the longest x1 0.84 us: advance(): block_volumes - COURANT * (interface[..., 1:, :] - interface[..., :-1, :])]
    ppermute x7 -> x9, starting transfers between devices: 12 us -> 13.2 us  [the longest x3 5.73 us: exchange(): block = jnp.concatenate([block, lax.ppermute(block, 'grp', route)], axis=0)]
    reshape x9 -> x0, local copies, waits for them, and re-layouts: 0.65 us -> none  [the longest x6 0.26 us: selected_lines(): flat = operand.reshape(operand.shape[0], -1)]
    broadcast_in_dim x1 -> x0, local copies, waits for them, and re-layouts: 0.62 us -> none  [local(): jnp.einsum('k,kfc->fc', matched, placed, precision=lax.Precision.HIGHEST)]
  transfers between devices with their start and end apart: 7 -> 9, of which waited for: 3 -> 7; matrix products, arithmetic and copies ran while one was open for 5% -> 0% of each run, Pallas kernels for 0% -> 0%
where the time goes in v1:
time: 32.8 us; the launch traced here: 32.3 us
  starting transfers between devices  13.2 us (40%)
  waiting for transfers between devices  10.4 us (32%)
  Pallas kernels  4.96 us (15%)
  local copies, waits for them, and re-layouts  3.08 us (9%)
  between operations  0.68 us (2%)
    ppermute x3, starting transfers between devices, exchange(): block = jnp.concatenate([block, lax.ppermute(block, 'grp', route)], axis=0)  5.73 us
    ppermute x3, starting transfers between devices, local(): early[k] = lax.ppermute(sent[k], 'dev', routes[k])  4.51 us
    ppermute x3, waiting for transfers between devices, exchange(): block = jnp.concatenate([block, lax.ppermute(block, 'grp', route)], axis=0)  4.32 us
    ppermute x3, waiting for transfers between devices, local(): late[k] = lax.ppermute(sent[count + k], 'dev', routes[k])  4.29 us
    unnamed x10, local copies, waits for them, and re-layouts  3.08 us
    ppermute x3, starting transfers between devices, local(): late[k] = lax.ppermute(sent[count + k], 'dev', routes[k])  2.91 us
    pallas_call x1, Pallas kernels, local(): pl.pallas_call(functools.partial(pack_kernel, n, slots, deltas), out_shap...  2.14 us
    pallas_call x1, Pallas kernels, local(): pl.pallas_call(functools.partial(step_kernel, n, slots, groups, butterfly...  1.86 us
  transfers between devices with their start and end apart: 9, of which 7 were waited for; matrix products, arithmetic and copies ran while one was open for 0% of the time, Pallas kernels for 0%

profile of v1, /device:TPU:0, one launch (start us, length us, event | category | flops | bytes accessed | tf_op | source)
XLA Modules:
  0.0 32.3 jit_solution(12052811164116378508)
XLA Ops:
  0.7 0.6 %copy-done.2 = s32[32]{0:T(128)S(1)} copy-done((s32[32]{0:T(128)S(1)}, s32[32]{0:T(128)}, u32[]{:S(2)}) %copy-start.2) | copy-done | bytes 152
  1.3 0.0 copy-done.1
  1.3 1.1 %copy-done = f32[8,5,4096]{2,0,1:T(8,128)S(1)} copy-done((f32[8,5,4096]{2,0,1:T(8,128)S(1)}, f32[8,5,4096]{2,0,1:T(8,128)}, u32[]{:S(2)}) %copy-start) | copy-done | bytes 655384
  2.4 0.7 %copy-done.3 = s32[32]{0:T(128)S(1)} copy-done((s32[32]{0:T(128)S(1)}, s32[32]{0:T(128)}, u32[]{:S(2)}) %copy-start.3) | copy-done | bytes 152
  3.1 2.1 %pack.1 = (f32[104,128]{1,0:T(8,128)S(1)}, f32[104,128]{1,0:T(8,128)S(1)}, f32[104,128]{1,0:T(8,128)S(1)}, f32[240,128]{1,0:T(8,128)S(1)}, f32[240,128]{1,0:T(8,...) custom-call(s32[32]{0:T(128)S(1)} %copy-done.2, ...), custom_call_target="tpu_custom_call" | custom-call | tf_op jit(solution)/shard_map/pack/pallas_call | solution.py:344
  5.2 0.5 %collective-permute-start = (f32[104,128]{1,0:T(8,128)S(1)}, f32[104,128]{1,0:T(8,128)S(1)}, u32[]{:S(2)}, u32[]{:S(2)}) collective-permute-start(f32[104,128]{1,0:T(8,128)S(1)} %get-tuple-element.16), channel_id=1, source_target_pairs={{0,1},{1,2},{2,3},{3,0},{4,5},{5,6},{6,7},{7,4},{8,9},{9,10},{10,1... | collective-permute-start | bytes 159752 | tf_op jit(solution)/shard_map/ppermute | solution.py:364
  5.8 2.6 %collective-permute-start.1 = (f32[104,128]{1,0:T(8,128)S(1)}, f32[104,128]{1,0:T(8,128)S(1)}, u32[]{:S(2)}, u32[]{:S(2)}) collective-permute-start(f32[104,128]{1,0:T(8,128)S(1)} %get-tuple-element.17), channel_id=1, source_target_pairs={{0,2},{1,3},{2,0},{3,1},{4,6},{5,7},{6,4},{7,5},{8,10},{9,11},{10,... | collective-permute-start | bytes 159752 | tf_op jit(solution)/shard_map/ppermute | solution.py:364
  8.3 1.4 %collective-permute-start.2 = (f32[104,128]{1,0:T(8,128)S(1)}, f32[104,128]{1,0:T(8,128)S(1)}, u32[]{:S(2)}, u32[]{:S(2)}) collective-permute-start(f32[104,128]{1,0:T(8,128)S(1)} %get-tuple-element.18), channel_id=1, source_target_pairs={{0,3},{1,0},{2,1},{3,2},{4,7},{5,4},{6,5},{7,6},{8,11},{9,8},{10,9... | collective-permute-start | bytes 159752 | tf_op jit(solution)/shard_map/ppermute | solution.py:364
  9.7 0.7 %collective-permute-done.1.refs_1_ = f32[104,128]{1,0:T(8,128)S(1)} collective-permute-done((f32[104,128]{1,0:T(8,128)S(1)}, f32[104,128]{1,0:T(8,128)S(1)}, u32[]{:S(2)}, u32[]{:S(2)}) %collective-permute-start.1) | collective-permute-done | bytes 53280 | tf_op jit(solution)/shard_map/ppermute | solution.py:364
  10.5 1.0 %collective-permute-done.2.refs_2_ = f32[104,128]{1,0:T(8,128)S(1)} collective-permute-done((f32[104,128]{1,0:T(8,128)S(1)}, f32[104,128]{1,0:T(8,128)S(1)}, u32[]{:S(2)}, u32[]{:S(2)}) %collective-permute-start.2) | collective-permute-done | bytes 53280 | tf_op jit(solution)/shard_map/ppermute | solution.py:364
  11.5 0.3 coarse.1
  11.8 1.6 %collective-permute-start.6 = (f32[16,128]{1,0:T(8,128)S(1)}, f32[16,128]{1,0:T(8,128)S(1)}, u32[]{:S(2)}, u32[]{:S(2)}) collective-permute-start(f32[16,128]{1,0:T(8,128)S(1)} %coarse.1), channel_id=1, source_target_pairs={{0,4},{4,0},{8,12},{12,8},{16,20},{20,16},{24,28},{28,24},{1,5},{5... | collective-permute-start | bytes 24584 | tf_op jit(solution)/shard_map/ppermute | solution.py:328
  13.3 2.2 %collective-permute-done.6 = f32[16,128]{1,0:T(8,128)S(1)} collective-permute-done((f32[16,128]{1,0:T(8,128)S(1)}, f32[16,128]{1,0:T(8,128)S(1)}, u32[]{:S(2)}, u32[]{:S(2)}) %collective-permute-start.6) | collective-permute-done | bytes 8224 | tf_op jit(solution)/shard_map/ppermute | solution.py:328
  15.5 1.6 %collective-permute-start.7 = (f32[32,128]{1,0:T(8,128)S(1)}, f32[32,128]{1,0:T(8,128)S(1)}, u32[]{:S(2)}, u32[]{:S(2)}) collective-permute-start(f32[32,128]{1,0:T(8,128)S(1)} %pad_maximum_fusion.2), channel_id=1, source_target_pairs={{0,8},{4,12},{8,0},{12,4},{16,24},{20,28},{24,16},{28,20},{1,9},{5... | collective-permute-start | bytes 49160 | tf_op jit(solution)/shard_map/ppermute | solution.py:328
  17.1 2.2 %collective-permute-done.7 = f32[32,128]{1,0:T(8,128)S(1)} collective-permute-done((f32[32,128]{1,0:T(8,128)S(1)}, f32[32,128]{1,0:T(8,128)S(1)}, u32[]{:S(2)}, u32[]{:S(2)}) %collective-permute-start.7) | collective-permute-done | bytes 16416 | tf_op jit(solution)/shard_map/ppermute | solution.py:328
  19.2 2.6 %collective-permute-start.8 = (f32[64,128]{1,0:T(8,128)S(1)}, f32[64,128]{1,0:T(8,128)S(1)}, u32[]{:S(2)}, u32[]{:S(2)}) collective-permute-start(f32[64,128]{1,0:T(8,128)S(1)} %pad_maximum_fusion.1), channel_id=1, source_target_pairs={{0,16},{4,20},{8,24},{12,28},{16,0},{20,4},{24,8},{28,12},{1,17},{... | collective-permute-start | bytes 98312 | tf_op jit(solution)/shard_map/ppermute | solution.py:328
  21.8 1.4 %collective-permute-start.4 = (f32[240,128]{1,0:T(8,128)S(1)}, f32[240,128]{1,0:T(8,128)S(1)}, u32[]{:S(2)}, u32[]{:S(2)}) collective-permute-start(f32[240,128]{1,0:T(8,128)S(1)} %get-tuple-element.20), channel_id=1, source_target_pairs={{0,2},{1,3},{2,0},{3,1},{4,6},{5,7},{6,4},{7,5},{8,10},{9,11},{10,... | collective-permute-start | bytes 368648 | tf_op jit(solution)/shard_map/ppermute | solution.py:366
  23.3 1.5 %collective-permute-start.5 = (f32[240,128]{1,0:T(8,128)S(1)}, f32[240,128]{1,0:T(8,128)S(1)}, u32[]{:S(2)}, u32[]{:S(2)}) collective-permute-start(f32[240,128]{1,0:T(8,128)S(1)} %get-tuple-element.21), channel_id=1, source_target_pairs={{0,3},{1,0},{2,1},{3,2},{4,7},{5,4},{6,5},{7,6},{8,11},{9,8},{10,9... | collective-permute-start | bytes 368648 | tf_op jit(solution)/shard_map/ppermute | solution.py:366
  24.8 2.1 %collective-permute-done.3.refs_3_ = f32[240,128]{1,0:T(8,128)S(1)} collective-permute-done((f32[240,128]{1,0:T(8,128)S(1)}, f32[240,128]{1,0:T(8,128)S(1)}, u32[]{:S(2)}, u32[]{:S(2)}) %collective-permute-start.3) | collective-permute-done | bytes 122912 | tf_op jit(solution)/shard_map/ppermute | solution.py:366
  26.9 1.2 %collective-permute-done.4.refs_4_ = f32[240,128]{1,0:T(8,128)S(1)} collective-permute-done((f32[240,128]{1,0:T(8,128)S(1)}, f32[240,128]{1,0:T(8,128)S(1)}, u32[]{:S(2)}, u32[]{:S(2)}) %collective-permute-start.4) | collective-permute-done | bytes 122912 | tf_op jit(solution)/shard_map/ppermute | solution.py:366
  28.0 1.0 %collective-permute-done.5.refs_5_ = f32[240,128]{1,0:T(8,128)S(1)} collective-permute-done((f32[240,128]{1,0:T(8,128)S(1)}, f32[240,128]{1,0:T(8,128)S(1)}, u32[]{:S(2)}, u32[]{:S(2)}) %collective-permute-start.5) | collective-permute-done | bytes 122912 | tf_op jit(solution)/shard_map/ppermute | solution.py:366
  29.1 0.7 %copy-done.4 = s32[1,32]{1,0:T(1,128)S(1)} copy-done((s32[1,32]{1,0:T(1,128)S(1)}, s32[1,32]{1,0:T(1,128)}, u32[]{:S(2)}) %copy-start.4) | copy-done | bytes 152
  29.7 1.9 %step.1 = (f32[5,32,4,128]{3,2,1,0:T(4,128)}, s32[16,128]{1,0:T(8,128)S(1)}) custom-call(s32[8]{0:T(128)S(1)} %get-tuple-element.13.plan, s32[1,32]{1,0:T(1,128)S(1)} %copy-done.4, f32[1280,128]{1,0:T(8,128)S(1)} %get-tuple-element.14.x, f32[240,128]{1,0:T(8,128)S(1)} %get-tuple-element.15.own.refs_3_, f32[104,128]{1,0:T(8,128)S(1)} %collective-permute-done.refs_0_, ...), custom_call_target="tpu_custom_call" | custom-call | tf_op jit(solution)/shard_map/step/pallas_call | solution.py:379
  31.6 0.7 %registers.1 = f32[5,1,256]{2,1,0:T(1,128)} custom-call(f32[128,128]{1,0:T(8,128)S(1)} %pad_maximum_fusion.faces, s32[16,128]{1,0:T(8,128)S(1)} %get-tuple-element.23.codes), custom_call_target="tpu_custom_call" | custom-call | tf_op jit(solution)/shard_map/registers/pallas_call | solution.py:391
  (11 shorter events, 0.0 us)
Async XLA Ops:
  0.6 0.7 %copy-start.2 = (s32[32]{0:T(128)S(1)}, s32[32]{0:T(128)}, u32[]{:S(2)}) copy-start(s32[32]{0:T(128)} %dev_hbm.1) | copy-start | bytes 388
  0.6 0.7 %copy-start.1 = (s32[2,16]{1,0:T(2,128)S(1)}, s32[2,16]{1,0:T(2,128)}, u32[]{:S(2)}) copy-start(s32[2,16]{1,0:T(2,128)} %nbr_hbm.1) | copy-start | bytes 388
  1.3 1.1 %copy-start = (f32[8,5,4096]{2,0,1:T(8,128)S(1)}, f32[8,5,4096]{2,0,1:T(8,128)}, u32[]{:S(2)}) copy-start(f32[8,5,4096]{2,0,1:T(8,128)} %param.5) | copy-start | bytes 1966084
  2.4 0.7 %copy-start.3 = (s32[32]{0:T(128)S(1)}, s32[32]{0:T(128)}, u32[]{:S(2)}) copy-start(s32[32]{0:T(128)} %slot_hbm.1) | copy-start | bytes 388
  5.2 4.5 %collective-permute-start = (f32[104,128]{1,0:T(8,128)S(1)}, f32[104,128]{1,0:T(8,128)S(1)}, u32[]{:S(2)}, u32[]{:S(2)}) collective-permute-start(f32[104,128]{1,0:T(8,128)S(1)} %get-tuple-element.16), channel_id=1, source_target_pairs={{0,1},{1,2},{2,3},{3,0},{4,5},{5,6},{6,7},{7,4},{8,9},{9,10},{10,1... | collective-permute-start | bytes 159752 | tf_op jit(solution)/shard_map/ppermute | solution.py:364
  5.8 4.7 %collective-permute-start.1 = (f32[104,128]{1,0:T(8,128)S(1)}, f32[104,128]{1,0:T(8,128)S(1)}, u32[]{:S(2)}, u32[]{:S(2)}) collective-permute-start(f32[104,128]{1,0:T(8,128)S(1)} %get-tuple-element.17), channel_id=1, source_target_pairs={{0,2},{1,3},{2,0},{3,1},{4,6},{5,7},{6,4},{7,5},{8,10},{9,11},{10,... | collective-permute-start | bytes 159752 | tf_op jit(solution)/shard_map/ppermute | solution.py:364
  8.3 3.2 %collective-permute-start.2 = (f32[104,128]{1,0:T(8,128)S(1)}, f32[104,128]{1,0:T(8,128)S(1)}, u32[]{:S(2)}, u32[]{:S(2)}) collective-permute-start(f32[104,128]{1,0:T(8,128)S(1)} %get-tuple-element.18), channel_id=1, source_target_pairs={{0,3},{1,0},{2,1},{3,2},{4,7},{5,4},{6,5},{7,6},{8,11},{9,8},{10,9... | collective-permute-start | bytes 159752 | tf_op jit(solution)/shard_map/ppermute | solution.py:364
  11.8 3.7 %collective-permute-start.6 = (f32[16,128]{1,0:T(8,128)S(1)}, f32[16,128]{1,0:T(8,128)S(1)}, u32[]{:S(2)}, u32[]{:S(2)}) collective-permute-start(f32[16,128]{1,0:T(8,128)S(1)} %coarse.1), channel_id=1, source_target_pairs={{0,4},{4,0},{8,12},{12,8},{16,20},{20,16},{24,28},{28,24},{1,5},{5... | collective-permute-start | bytes 24584 | tf_op jit(solution)/shard_map/ppermute | solution.py:328
  15.5 3.7 %collective-permute-start.7 = (f32[32,128]{1,0:T(8,128)S(1)}, f32[32,128]{1,0:T(8,128)S(1)}, u32[]{:S(2)}, u32[]{:S(2)}) collective-permute-start(f32[32,128]{1,0:T(8,128)S(1)} %pad_maximum_fusion.2), channel_id=1, source_target_pairs={{0,8},{4,12},{8,0},{12,4},{16,24},{20,28},{24,16},{28,20},{1,9},{5... | collective-permute-start | bytes 49160 | tf_op jit(solution)/shard_map/ppermute | solution.py:328
  19.2 5.5 %collective-permute-start.8 = (f32[64,128]{1,0:T(8,128)S(1)}, f32[64,128]{1,0:T(8,128)S(1)}, u32[]{:S(2)}, u32[]{:S(2)}) collective-permute-start(f32[64,128]{1,0:T(8,128)S(1)} %pad_maximum_fusion.1), channel_id=1, source_target_pairs={{0,16},{4,20},{8,24},{12,28},{16,0},{20,4},{24,8},{28,12},{1,17},{... | collective-permute-start | bytes 98312 | tf_op jit(solution)/shard_map/ppermute | solution.py:328
  21.8 5.0 %collective-permute-start.3 = (f32[240,128]{1,0:T(8,128)S(1)}, f32[240,128]{1,0:T(8,128)S(1)}, u32[]{:S(2)}, u32[]{:S(2)}) collective-permute-start(f32[240,128]{1,0:T(8,128)S(1)} %get-tuple-element.19), channel_id=1, source_target_pairs={{0,1},{1,2},{2,3},{3,0},{4,5},{5,6},{6,7},{7,4},{8,9},{9,10},{10,1... | collective-permute-start | bytes 368648 | tf_op jit(solution)/shard_map/ppermute | solution.py:366
  21.8 6.2 %collective-permute-start.4 = (f32[240,128]{1,0:T(8,128)S(1)}, f32[240,128]{1,0:T(8,128)S(1)}, u32[]{:S(2)}, u32[]{:S(2)}) collective-permute-start(f32[240,128]{1,0:T(8,128)S(1)} %get-tuple-element.20), channel_id=1, source_target_pairs={{0,2},{1,3},{2,0},{3,1},{4,6},{5,7},{6,4},{7,5},{8,10},{9,11},{10,... | collective-permute-start | bytes 368648 | tf_op jit(solution)/shard_map/ppermute | solution.py:366
  23.3 5.8 %collective-permute-start.5 = (f32[240,128]{1,0:T(8,128)S(1)}, f32[240,128]{1,0:T(8,128)S(1)}, u32[]{:S(2)}, u32[]{:S(2)}) collective-permute-start(f32[240,128]{1,0:T(8,128)S(1)} %get-tuple-element.21), channel_id=1, source_target_pairs={{0,3},{1,0},{2,1},{3,2},{4,7},{5,4},{6,5},{7,6},{8,11},{9,8},{10,9... | collective-permute-start | bytes 368648 | tf_op jit(solution)/shard_map/ppermute | solution.py:366
  29.1 0.7 %copy-start.4 = (s32[1,32]{1,0:T(1,128)S(1)}, s32[1,32]{1,0:T(1,128)}, u32[]{:S(2)}) copy-start(s32[1,32]{1,0:T(1,128)} %cmap.1) | copy-start | bytes 388
